TPU v7x, 32 devices: a whole 2x2x4 slice. The times are simulated.
32 devices in a mesh: leaf: 16 (over z, y, x), col: 2 (over core).
Axes of the slice: x: 2, y: 2, z: 4, core: 2. Of those that a mesh axis runs over, the one named last changes fastest.
Arguments:
- sources: bfloat16 [65536, 256], P('leaf', 'col'), may hold values from -6 to 6
- near_tiles: bfloat16 [256, 8, 256, 256], P('leaf', 'col'), may hold values from -0.125 to 0.125
- near_index: int32 [256, 8], P('leaf'), may hold values from 0 to 255, as said below
- near_count: int32 [256], P('leaf'), may hold values from 1 to 8, as said below
- leaf_basis: bfloat16 [256, 64, 256], P('leaf'), may hold values from -0.375 to 0.375
- leaf_coupling: bfloat16 [256, 64, 256], P('leaf'), may hold values from -0.375 to 0.375
- leaf_far: int32 [256, 4], P('leaf'), may hold values from 0 to 255, as said below
- up_leaf: bfloat16 [32, 64, 512], P('leaf'), may hold values from -0.25 to 0.25
- mid_coupling: bfloat16 [32, 64, 256], P('leaf'), may hold values from -0.375 to 0.375
- mid_far: int32 [32, 4], P('leaf'), may hold values from 0 to 31, as said below
- up_mid: bfloat16 [32, 64, 64], P('leaf'), may hold values from -0.75 to 0.75
- top_coupling: bfloat16 [4, 64, 256], replicated, may hold values from -0.4375 to 0.4375
Outputs:
- product: float32 [65536, 256], P('leaf', 'col')
Inputs may be any that keep to these rules, and one draw needn't show every extreme that they name: `near_index`: entry 0 of row i is i; the other 7 entries are distinct leaves j with j != i and |i - j| <= 8. Only the first near_count[i] slots of leaf i count; some leaf has all 8. `leaf_far`: row i holds 4 distinct leaves j != i with |i // 8 - j // 8| <= 1. `mid_far`: row a holds 4 distinct middle clusters b != a with |a // 8 - b // 8| <= 1.
All inputs are finite; a program needn't handle non-finite values.
Results may differ from a plain program's by a relative error of at most 0.01.
Values may be sent and summed in bfloat16 or wider, within the bound.
No kernel may reach another device: no remote copies, remote signals or barrier semaphores. Data moves between devices by JAX's collectives and lax.ppermute only.
A program may use at most 128 MiB of HBM per device.

v0:
```python
import jax
import jax.numpy as jnp
from jax import lax
from jax.sharding import PartitionSpec as P

CHILD = 8
FAR = 4


def padded(x, sides, width):
    for axis, dim in sides:
        size, length = (lax.axis_size(axis), x.shape[dim])
        up = [(i, (i + 1) % size) for i in range(size - 1)]
        down = [(j, i) for i, j in up]
        last = lax.slice_in_dim(x, length - width, length, axis=dim)
        first = lax.slice_in_dim(x, 0, width, axis=dim)
        before = lax.ppermute(last, axis, up)
        after = lax.ppermute(first, axis, down)
        x = jnp.concatenate([before, x, after], axis=dim)
    return x


def shards(
    sources,
    near_tiles,
    near_index,
    near_count,
    leaf_basis,
    leaf_coupling,
    leaf_far,
    up_leaf,
    mid_coupling,
    mid_far,
    up_mid,
    top_coupling,
):
    f32 = jnp.float32
    bf16 = jnp.bfloat16
    leaf_count = leaf_basis.shape[0]
    rank_size = leaf_basis.shape[1]
    leaf_size = leaf_basis.shape[2]
    col_count = sources.shape[1]
    mid_count = leaf_count // CHILD
    total_top = top_coupling.shape[0]
    device = lax.axis_index("leaf")
    first_leaf = device * leaf_count
    first_mid = device * mid_count
    window = padded(sources, (("leaf", 0),), CHILD * leaf_size)
    near_local = near_index - (first_leaf - CHILD)
    all_tiles = lax.all_gather(near_tiles, "col", axis=1, tiled=True)
    slot_count = all_tiles.shape[1]
    blocks = window.reshape(-1, leaf_size, window.shape[1])
    picked = blocks[near_local]
    live_mask = jnp.arange(slot_count)[None, :] < near_count[:, None]
    picked = jnp.where(live_mask[:, :, None, None], picked, jnp.zeros((), bf16))
    result = jnp.einsum("lsij,lsjc->lic", all_tiles, picked, preferred_element_type=f32)
    near_part = result.reshape(leaf_count * leaf_size, window.shape[1])
    leaf_blocks = sources.reshape(leaf_count, leaf_size, col_count)
    leaf_coef = jnp.einsum(
        "lrk,lkc->lrc", leaf_basis, leaf_blocks, preferred_element_type=f32
    ).astype(bf16)
    mid_coef = jnp.einsum(
        "qrk,qkc->qrc",
        up_leaf,
        leaf_coef.reshape(mid_count, CHILD * rank_size, col_count),
        preferred_element_type=f32,
    ).astype(bf16)
    mid_lift = jnp.einsum("qrs,qsc->qrc", up_mid, mid_coef, preferred_element_type=f32).astype(bf16)
    parent = (first_mid + jnp.arange(mid_count)) // CHILD
    mid_flat = mid_far.reshape(-1)
    top_range = jnp.arange(total_top)
    coef_piece = lax.all_gather(mid_coef, "leaf", axis=0, tiled=True)
    lift_piece = lax.all_gather(mid_lift, "leaf", axis=0, tiled=True)
    global_ids = jnp.arange(coef_piece.shape[0])
    group_map = (top_range[:, None] == (global_ids // CHILD)[None, :]).astype(bf16)
    top_total = jnp.einsum("pk,krc->prc", group_map, lift_piece, preferred_element_type=f32)
    global_ids = jnp.arange(coef_piece.shape[0])
    pick_map = (mid_flat[:, None] == global_ids[None, :]).astype(bf16)
    mid_picked = jnp.einsum("ik,krc->irc", pick_map, coef_piece, preferred_element_type=f32)
    top_coef = top_total.astype(bf16)
    parent_rows = top_coupling[parent]
    keep_mask = top_range[None, :] != parent[:, None]
    stacked = jnp.where(keep_mask[:, :, None, None], top_coef[None], jnp.zeros((), bf16))
    top_field = jnp.einsum(
        "qrk,qkc->qrc",
        parent_rows,
        stacked.reshape(mid_count, total_top * rank_size, col_count),
        preferred_element_type=f32,
    ).astype(bf16)
    mid_chosen = mid_picked.astype(bf16).reshape(mid_count, FAR * rank_size, col_count)
    mid_field = (
        jnp.einsum("qrk,qkc->qrc", mid_coupling, mid_chosen, preferred_element_type=f32)
        + jnp.einsum("qrs,qrc->qsc", up_mid, top_field, preferred_element_type=f32)
    ).astype(bf16)
    leaf_window = padded(leaf_coef, (("leaf", 0),), CHILD)
    far_local = leaf_far - (first_leaf - CHILD)
    leaf_chosen = leaf_window[far_local].reshape(leaf_count, FAR * rank_size, col_count)
    down_part = jnp.einsum("qrs,qrc->qsc", up_leaf, mid_field, preferred_element_type=f32).reshape(
        leaf_count, rank_size, col_count
    )
    leaf_field = (
        jnp.einsum("lrk,lkc->lrc", leaf_coupling, leaf_chosen, preferred_element_type=f32)
        + down_part
    ).astype(bf16)
    far_part = jnp.einsum(
        "lrk,lrc->lkc", leaf_basis, leaf_field, preferred_element_type=f32
    ).reshape(leaf_count * leaf_size, col_count)
    return near_part + far_part


def solution(mesh):
    return jax.shard_map(
        shards,
        mesh=mesh,
        in_specs=(
            P("leaf", "col"),
            P("leaf", "col", None, None),
            P("leaf", None),
            P("leaf"),
            P("leaf", None, None),
            P("leaf", None, None),
            P("leaf", None),
            P("leaf", None, None),
            P("leaf", None, None),
            P("leaf", None),
            P("leaf", None, None),
            P(),
        ),
        out_specs=P("leaf", "col"),
        check_vma=False,
    )
```

profile of v0, /device:TPU:0, one launch (start us, length us, event | category | flops | bytes accessed | tf_op | source)
XLA Modules:
  0.0 168.7 jit_solution(13844385451105794318)
XLA Ops:
  6.5 0.0 copy-start
  6.5 0.0 copy-start.1
  6.5 0.0 all-gather.2.cloned.1.call-start
  6.5 0.7 all-gather.2.cloned.1.call-update
  7.3 0.0 copy-start.9
  7.3 0.0 copy-start.4
  7.3 0.0 copy-start.6
  7.3 0.0 copy-start.11
  7.3 0.0 copy-start.7
  7.3 0.0 copy-start.10
  7.3 0.0 copy-start.8
  7.3 0.0 copy-start.5
  7.3 0.2 copy-done
  7.6 0.3 copy-done.1
  7.9 0.3 convolution_convert_fusion
  8.3 4.9 %collective-permute-start.2 = (bf16[8,64,128]{2,1,0:T(8,128)(2,1)S(1)}, bf16[8,64,128]{2,1,0:T(8,128)(2,1)S(1)}, u32[]{:S(2)}, u32[]{:S(2)}) collective-permute-start(bf16[8,64,128]{2,1,0:T(8,128)(2,1)S(1)} %get-tuple-element.7), channel_id=1, source_target_pairs={{0,2},{2,4},{4,6},{6,8},{8,10},{10,12},{12,14},{14,16},{16,18},{18... | collective-permute-start | bytes 393224 | tf_op jit(solution)/shard_map/ppermute | solution.py:17
  13.2 1.3 collective-permute-start.3
  14.5 1.1 fusion.33
  15.5 5.4 %collective-permute-start = (bf16[2048,128]{1,0:T(8,128)(2,1)}, bf16[2048,128]{1,0:T(8,128)(2,1)}, u32[]{:S(2)}, u32[]{:S(2)}) collective-permute-start(bf16[2048,128]{1,0:T(8,128)(2,1)} %get-tuple-element.5), channel_id=1, source_target_pairs={{0,2},{2,4},{4,6},{6,8},{8,10},{10,12},{12,14},{14,16},{16,18},{18... | collective-permute-start | bytes 1572872 | tf_op jit(solution)/shard_map/ppermute | solution.py:17
  20.9 1.3 collective-permute-start.1
  22.2 0.0 copy-done.9
  22.2 0.1 copy.27
  22.3 0.1 reshape.160
  22.4 0.0 copy-done.4
  22.4 0.2 convolution_convert_fusion.5
  22.6 0.0 copy-done.6
  22.6 0.1 fusion.12
  22.7 0.0 copy-start.3
  22.7 57.8 %all_gather.11 = bf16[32,64,128]{2,1,0:T(8,128)(2,1)S(1)} all-gather(bf16[2,64,128]{2,1,0:T(8,128)(2,1)S(1)} %fusion.12), channel_id=1, replica_groups=mesh['leaf'=16,'col'=2] {'leaf'}, dimensions={0}, use_global_device_ids=true | all-gather | bytes 557056 | tf_op jit(solution)/shard_map/all_gather | solution.py:73
  80.5 0.4 convolution_convert_fusion.2
  80.9 0.1 iota_compare_fusion.3
  81.0 0.1 broadcast_in_dim.59
  81.1 0.1 broadcast_in_dim.60
  81.2 0.0 copy-done.11
  81.2 0.1 eq.28
  81.3 38.7 %all_gather.10 = bf16[32,64,128]{2,1,0:T(8,128)(2,1)S(1)} all-gather(bf16[2,64,128]{2,1,0:T(8,128)(2,1)S(1)} %bitcast.59), channel_id=1, replica_groups=mesh['leaf'=16,'col'=2] {'leaf'}, dimensions={0}, use_global_device_ids=true | all-gather | bytes 557056 | tf_op jit(solution)/shard_map/all_gather | solution.py:72
  119.9 0.4 convolution_convert_fusion.1
  120.4 0.0 copy-done.7
  120.4 0.6 gather_fusion.2
  121.0 0.0 copy-done.10
  121.0 0.1 iota_compare_fusion
  121.1 0.0 copy-done.8
  121.1 0.4 fusion.11
  121.5 0.0 copy-done.5
  121.5 0.4 convolution_bitcast_fusion.1
  121.9 0.1 copy.25
  122.0 0.1 reshape.152
  122.1 0.2 copy.33
  122.3 0.0 collective-permute-done.2
  122.3 0.0 collective-permute-done.3
  122.3 1.0 pad_maximum_fusion.1
  123.3 0.7 gather_fusion.1
  124.0 0.0 copy-done.3
  124.0 1.9 %fusion.9 = f32[16,128,256]{2,1,0:T(8,128)} fusion(bf16[16,64,256]{2,1,0:T(8,128)(2,1)S(1)} %copy-done, f32[16,64,128]{2,1,0:T(8,128)S(1)} %bitcast.57, bf16[16,64,256]{2,1,0:T(8,128)(2,1)S(1)} %copy-done.3, bf16[16,256,128]{2,1,0:T(8,128)(2,1)S(1)} %bitcast.56), kind=kOutput, calls=%fused_computation.15 | convolution fusion | flops 134479872 | bytes 4718592 | tf_op jit(solution)/shard_map/lrk,lrc->lkc/dot_general | solution.py:105
  126.0 0.0 collective-permute-done
  126.0 0.0 collective-permute-done.1
  126.0 1.7 pad_maximum_fusion
  127.6 6.6 %gather_fusion = bf16[128,256,128]{2,1,0:T(8,128)(2,1)} fusion(bf16[32,256,128]{2,1,0:T(8,128)(2,1)S(1)} %bitcast.52, s32[1024]{0:T(1024)S(1)} %pad_clamp_fusion.2), kind=kCustom, calls=%fused_computation | custom fusion | bytes 16777728 | tf_op jit(solution)/shard_map/gather | solution.py:53
  134.2 0.0 copy-start.2
  134.2 12.1 %copy.26 = bf16[128,256,128]{1,2,0:T(8,128)(2,1)} copy(bf16[128,256,128]{2,1,0:T(8,128)(2,1)} %gather_fusion) | data formatting | bytes 16777216 | tf_op jit(solution)/shard_map/gather | solution.py:53
  146.3 0.0 all-gather.2.cloned.1.call-done
  146.3 0.0 copy-done.2
  146.3 12.7 %fusion.4 = f32[16,256,128]{1,2,0:T(8,128)} fusion(f32[16,128,256]{2,1,0:T(8,128)S(1)} %copy-done.2, bf16[16,8,256,256]{3,2,1,0:T(8,128)(2,1)} %all-gather.2.cloned.1.call-done, bf16[16,8,256,128]{2,3,1,0:T(8,128)(2,1)} %bitcast.54, pred[16,8]{1,0:T(8,128)(4,1)S(1)} %iota_compare_fusion), kind=kOutput, calls=%fused_computation.9 | convolution fusion | flops 2152202240 | bytes 29360256 | tf_op jit(solution)/shard_map/lsij,lsjc->lic/dot_general | solution.py:56
  159.0 2.9 %copy.34 = f32[16,256,128]{2,1,0:T(8,128)} copy(f32[16,256,128]{1,2,0:T(8,128)} %fusion.4) | data formatting | bytes 4194304 | tf_op jit(solution)/shard_map/add | solution.py:108
  (11 shorter events, 0.1 us)
Async XLA Ops:
  6.5 1.0 copy-start
  6.5 1.4 copy-start.1
  6.5 139.8 %all-gather.2.cloned.1.call-start = ((), (), s32[]{:S(2)}) async-start(), calls=%async_computation | async-start | bytes 25165824 | tf_op jit(solution)/shard_map/all_gather | solution.py:50
  7.3 14.9 %copy-start.9 = (s32[16,4]{0,1:T(4,128)S(1)}, s32[16,4]{0,1:T(4,128)}, u32[]{:S(2)}) copy-start(s32[16,4]{0,1:T(4,128)} %param.18) | copy-start | bytes 772
  7.3 15.1 %copy-start.4 = (bf16[2,64,512]{2,1,0:T(8,128)(2,1)S(1)}, bf16[2,64,512]{2,1,0:T(8,128)(2,1)}, u32[]{:S(2)}) copy-start(bf16[2,64,512]{2,1,0:T(8,128)(2,1)} %param.19) | copy-start | bytes 393220
  7.3 15.3 %copy-start.6 = (bf16[2,64,64]{2,1,0:T(8,128)(2,1)S(1)}, bf16[2,64,64]{2,1,0:T(8,128)(2,1)}, u32[]{:S(2)}) copy-start(bf16[2,64,64]{2,1,0:T(8,128)(2,1)} %param.22) | copy-start | bytes 49156
  7.3 73.9 %copy-start.11 = (s32[2,4]{1,0:T(2,128)S(1)}, s32[2,4]{1,0:T(2,128)}, u32[]{:S(2)}) copy-start(s32[2,4]{1,0:T(2,128)} %param.21) | copy-start | bytes 100
  7.3 113.1 %copy-start.7 = (bf16[4,64,256]{2,1,0:T(8,128)(2,1)S(1)}, bf16[4,64,256]{2,1,0:T(8,128)(2,1)}, u32[]{:S(2)}) copy-start(bf16[4,64,256]{2,1,0:T(8,128)(2,1)} %param.23) | copy-start | bytes 393220
  7.3 113.7 %copy-start.10 = (s32[16]{0:T(128)S(1)}, s32[16]{0:T(128)}, u32[]{:S(2)}) copy-start(s32[16]{0:T(128)} %param.15) | copy-start | bytes 196
  7.3 113.7 %copy-start.8 = (s32[16,8]{0,1:T(8,128)S(1)}, s32[16,8]{0,1:T(8,128)}, u32[]{:S(2)}) copy-start(s32[16,8]{0,1:T(8,128)} %param.14) | copy-start | bytes 1540
  7.3 114.1 %copy-start.5 = (bf16[2,64,256]{2,1,0:T(8,128)(2,1)S(1)}, bf16[2,64,256]{2,1,0:T(8,128)(2,1)}, u32[]{:S(2)}) copy-start(bf16[2,64,256]{2,1,0:T(8,128)(2,1)} %param.20) | copy-start | bytes 196612
  8.3 114.0 %collective-permute-start.2 = (bf16[8,64,128]{2,1,0:T(8,128)(2,1)S(1)}, bf16[8,64,128]{2,1,0:T(8,128)(2,1)S(1)}, u32[]{:S(2)}, u32[]{:S(2)}) collective-permute-start(bf16[8,64,128]{2,1,0:T(8,128)(2,1)S(1)} %get-tuple-element.7), channel_id=1, source_target_pairs={{0,2},{2,4},{4,6},{6,8},{8,10},{10,12},{12,14},{14,16},{16,18},{18... | collective-permute-start | bytes 393224 | tf_op jit(solution)/shard_map/ppermute | solution.py:17
  13.2 109.1 %collective-permute-start.3 = (bf16[8,64,128]{2,1,0:T(8,128)(2,1)S(1)}, bf16[8,64,128]{2,1,0:T(8,128)(2,1)}, u32[]{:S(2)}, u32[]{:S(2)}) collective-permute-start(bf16[8,64,128]{2,1,0:T(8,128)(2,1)S(1)} %get-tuple-element.8), channel_id=1, source_target_pairs={{2,0},{4,2},{6,4},{8,6},{10,8},{12,10},{14,12},{16,14},{18,16},{20... | collective-permute-start | bytes 393224 | tf_op jit(solution)/shard_map/ppermute | solution.py:18
  15.5 110.4 %collective-permute-start = (bf16[2048,128]{1,0:T(8,128)(2,1)}, bf16[2048,128]{1,0:T(8,128)(2,1)}, u32[]{:S(2)}, u32[]{:S(2)}) collective-permute-start(bf16[2048,128]{1,0:T(8,128)(2,1)} %get-tuple-element.5), channel_id=1, source_target_pairs={{0,2},{2,4},{4,6},{6,8},{8,10},{10,12},{12,14},{14,16},{16,18},{18... | collective-permute-start | bytes 1572872 | tf_op jit(solution)/shard_map/ppermute | solution.py:17
  20.9 105.1 %collective-permute-start.1 = (bf16[2048,128]{1,0:T(8,128)(2,1)}, bf16[2048,128]{1,0:T(8,128)(2,1)}, u32[]{:S(2)}, u32[]{:S(2)}) collective-permute-start(bf16[2048,128]{1,0:T(8,128)(2,1)} %get-tuple-element.6), channel_id=1, source_target_pairs={{2,0},{4,2},{6,4},{8,6},{10,8},{12,10},{14,12},{16,14},{18,16},{20... | collective-permute-start | bytes 1572872 | tf_op jit(solution)/shard_map/ppermute | solution.py:18
  22.7 101.3 %copy-start.3 = (bf16[16,64,256]{2,1,0:T(8,128)(2,1)S(1)}, bf16[16,64,256]{2,1,0:T(8,128)(2,1)}, u32[]{:S(2)}) copy-start(bf16[16,64,256]{2,1,0:T(8,128)(2,1)} %param.17) | copy-start | bytes 1572868
  134.2 12.1 %copy-start.2 = (f32[16,128,256]{2,1,0:T(8,128)S(1)}, f32[16,128,256]{2,1,0:T(8,128)}, u32[]{:S(2)}) copy-start(f32[16,128,256]{2,1,0:T(8,128)} %fusion.9) | copy-start | bytes 6291460
Sparse Core Ops, SparseCore 0:
  8.9 32.7 all-gather.1
where the time goes:
time: 169 us
  blocking collectives  96.5 us (57%)
  local copies, waits for them, and re-layouts  25.4 us (15%)
  matrix products  16.8 us (10%)
  between operations  13.7 us (8%)
  starting transfers between devices  12.8 us (8%)
  other arithmetic  2.82 us (2%)
    all_gather x1, blocking collectives, shards(): lift_piece = lax.all_gather(mid_lift, 'leaf', axis=0, tiled=True)  57.8 us
    all_gather x1, blocking collectives, shards(): coef_piece = lax.all_gather(mid_coef, 'leaf', axis=0, tiled=True)  38.7 us
    gather x2, local copies, waits for them, and re-layouts, shards(): picked = blocks[near_local]  18.7 us
    dot_general x1, matrix products, shards(): jnp.einsum('lsij,lsjc->lic', all_tiles, picked, preferred_element_type=f32)  12.7 us
    ppermute x2, starting transfers between devices, padded(): before = lax.ppermute(last, axis, up)  10.2 us
  transfers between devices with their start and end apart: 5, of which 0 were waited for; matrix products, arithmetic and copies ran while one was open for 17% of the time, Pallas kernels for 0%

commit v1 on v0

--- a/solution.py
+++ b/solution.py
@@ -2,9 +2,13 @@
 import jax.numpy as jnp
 from jax import lax
 from jax.sharding import PartitionSpec as P
+from jax.lax import all_gather
 
 CHILD = 8
 FAR = 4
+meet_circles_here = lambda xin, v0: jnp.split(
+    all_gather(jnp.concatenate([xin, v0], 1), "leaf", axis=0, tiled=True), [xin.shape[1]], 1
+)
 
 
 def padded(x, sides, width):
@@ -69,8 +73,7 @@
     parent = (first_mid + jnp.arange(mid_count)) // CHILD
     mid_flat = mid_far.reshape(-1)
     top_range = jnp.arange(total_top)
-    coef_piece = lax.all_gather(mid_coef, "leaf", axis=0, tiled=True)
-    lift_piece = lax.all_gather(mid_lift, "leaf", axis=0, tiled=True)
+    coef_piece, lift_piece = meet_circles_here(mid_coef, mid_lift)
     global_ids = jnp.arange(coef_piece.shape[0])
     group_map = (top_range[:, None] == (global_ids // CHILD)[None, :]).astype(bf16)
     top_total = jnp.einsum("pk,krc->prc", group_map, lift_piece, preferred_element_type=f32)

time: 169 us -> 123 us (0.73)
  blocking collectives: 96.5 us -> 0 us
  waiting for transfers between devices: 0.72 us -> 44 us
  local copies, waits for them, and re-layouts: 25.4 us -> 28.9 us
  matrix products: 16.8 us -> 18.9 us
    all_gather x2 -> x0, blocking collectives: 96.5 us -> none  [the longest x1 57.8 us: shards(): lift_piece = lax.all_gather(mid_lift, 'leaf', axis=0, tiled=True)]
    all_gather x1, waiting for transfers between devices: 0.01 us -> 25.2 us  [shards(): all_tiles = lax.all_gather(near_tiles, 'col', axis=1, tiled=True)]
    ppermute x2, waiting for transfers between devices: 0.01 us -> 17.7 us  [padded(): before = lax.ppermute(last, axis, up)]
  transfers between devices with their start and end apart: 5 -> 6, of which waited for: 0 -> 3; matrix products, arithmetic and copies ran while one was open for 17% -> 27% of each run, Pallas kernels for 0% -> 0%
where the time goes in v1:
time: 123 us; the launch traced here: 122 us
  waiting for transfers between devices  44 us (36%)
  local copies, waits for them, and re-layouts  28.9 us (23%)
  matrix products  18.9 us (15%)
  between operations  13.7 us (11%)
  starting transfers between devices  12.7 us (10%)
  other arithmetic  3.97 us (3%)
    all_gather x1, waiting for transfers between devices, shards(): all_tiles = lax.all_gather(near_tiles, 'col', axis=1, tiled=True)  25.2 us
    gather x2, local copies, waits for them, and re-layouts, shards(): picked = blocks[near_local]  18.7 us
    ppermute x2, waiting for transfers between devices, padded(): before = lax.ppermute(last, axis, up)  17.7 us
    dot_general x1, matrix products, shards(): jnp.einsum('lsij,lsjc->lic', all_tiles, picked, preferred_element_type=f32)  11.9 us
    ppermute x2, starting transfers between devices, padded(): before = lax.ppermute(last, axis, up)  10.1 us
    ppermute x2, starting transfers between devices, padded(): after = lax.ppermute(first, axis, down)  2.57 us
    concatenate x2, other arithmetic, padded(): x = jnp.concatenate([before, x, after], axis=dim)  2.56 us
  transfers between devices with their start and end apart: 6, of which 3 were waited for; matrix products, arithmetic and copies ran while one was open for 27% of the time, Pallas kernels for 0%

profile of v1, /device:TPU:0, one launch (start us, length us, event | category | flops | bytes accessed | tf_op | source)
XLA Modules:
  0.0 122.2 jit_solution(16972553186238301732)
XLA Ops:
  6.5 0.0 copy-start
  6.5 0.0 all-gather.5.cloned.1.call-start
  6.5 1.0 copy-done
  7.6 1.5 %convolution_convert_fusion = bf16[16,64,128]{2,1,0:T(8,128)(2,1)S(1)} fusion(bf16[16,64,256]{2,1,0:T(8,128)(2,1)S(1)} %copy-done, bf16[16,256,128]{2,1,0:T(8,128)(2,1)} %bitcast.53), kind=kOutput, calls=%fused_computation.14 | convolution fusion | flops 67239936 | bytes 1835008 | tf_op jit(solution)/shard_map/lrk,lkc->lrc/dot_general | solution.py:63
  9.1 1.1 convolution_convert_fusion.5
  10.2 0.9 fusion.12
  11.1 0.6 pad_maximum_fusion.2
  11.7 0.0 all-gather.5.cloned.1.call-update
  11.8 0.0 copy-start.1
  11.8 0.0 copy-start.9
  11.8 0.0 copy-start.10
  11.8 0.0 copy-start.8
  11.8 0.0 all-gather.3.cloned.1.call-start
  11.9 0.7 all-gather.3.cloned.1.call-update
  12.6 0.7 fusion.35
  13.2 5.5 %collective-permute-start.2 = (bf16[8,64,128]{2,1,0:T(8,128)(2,1)}, bf16[8,64,128]{2,1,0:T(8,128)(2,1)}, u32[]{:S(2)}, u32[]{:S(2)}) collective-permute-start(bf16[8,64,128]{2,1,0:T(8,128)(2,1)} %get-tuple-element.9), channel_id=1, source_target_pairs={{0,2},{2,4},{4,6},{6,8},{8,10},{10,12},{12,14},{14,16},{16,18},{18... | collective-permute-start | bytes 393224 | tf_op jit(solution)/shard_map/ppermute | solution.py:21
  18.8 1.3 %collective-permute-start.3 = (bf16[8,64,128]{2,1,0:T(8,128)(2,1)S(1)}, bf16[8,64,128]{2,1,0:T(8,128)(2,1)}, u32[]{:S(2)}, u32[]{:S(2)}) collective-permute-start(bf16[8,64,128]{2,1,0:T(8,128)(2,1)S(1)} %get-tuple-element.10), channel_id=1, source_target_pairs={{2,0},{4,2},{6,4},{8,6},{10,8},{12,10},{14,12},{16,14},{18,16},{20... | collective-permute-start | bytes 393224 | tf_op jit(solution)/shard_map/ppermute | solution.py:22
  20.0 0.0 copy-done.1
  20.1 0.1 fusion.33
  20.1 4.6 %collective-permute-start = (bf16[2048,128]{1,0:T(8,128)(2,1)S(1)}, bf16[2048,128]{1,0:T(8,128)(2,1)S(1)}, u32[]{:S(2)}, u32[]{:S(2)}) collective-permute-start(bf16[2048,128]{1,0:T(8,128)(2,1)S(1)} %get-tuple-element.5), channel_id=1, source_target_pairs={{0,2},{2,4},{4,6},{6,8},{8,10},{10,12},{12,14},{14,16},{16,18},{18... | collective-permute-start | bytes 1572872 | tf_op jit(solution)/shard_map/ppermute | solution.py:21
  24.7 1.3 %collective-permute-start.1 = (bf16[2048,128]{1,0:T(8,128)(2,1)S(1)}, bf16[2048,128]{1,0:T(8,128)(2,1)}, u32[]{:S(2)}, u32[]{:S(2)}) collective-permute-start(bf16[2048,128]{1,0:T(8,128)(2,1)S(1)} %get-tuple-element.6), channel_id=1, source_target_pairs={{2,0},{4,2},{6,4},{8,6},{10,8},{12,10},{14,12},{16,14},{18,16},{20... | collective-permute-start | bytes 1572872 | tf_op jit(solution)/shard_map/ppermute | solution.py:22
  26.0 0.0 copy-done.9
  26.0 0.1 copy.29
  26.1 0.1 reshape.160
  26.3 0.0 copy-done.10
  26.3 0.1 iota_compare_fusion
  26.4 0.0 copy-done.8
  26.4 0.1 iota_compare_fusion.3
  26.4 0.6 and_select_fusion
  27.0 0.1 broadcast_in_dim.59
  27.1 0.1 broadcast_in_dim.60
  27.2 0.8 eq.28
  27.9 0.1 copy.27
  28.0 0.1 reshape.152
  28.1 2.1 %gather_fusion.2 = bf16[2,64,256]{2,1,0:T(8,128)(2,1)} fusion(bf16[4,64,256]{2,1,0:T(8,128)(2,1)} %param.23, s32[1024]{0:T(1024)S(1)} %pad_clamp_fusion), kind=kCustom, calls=%fused_computation.2 | custom fusion | bytes 131080 | tf_op jit(solution)/shard_map/gather | solution.py:84
  30.2 0.0 collective-permute-done.2
  30.2 0.0 collective-permute-done.3
  30.2 1.0 pad_maximum_fusion.1
  31.2 1.7 %gather_fusion.1 = bf16[64,64,128]{2,1,0:T(8,128)(2,1)} fusion(bf16[32,64,128]{2,1,0:T(8,128)(2,1)S(1)} %pad_maximum_fusion.1, s32[1024]{0:T(1024)S(1)} %pad_clamp_fusion.1), kind=kCustom, calls=%fused_computation.1 | custom fusion | bytes 2097408 | tf_op jit(solution)/shard_map/gather | solution.py:100
  32.9 17.7 %collective-permute-done = bf16[2048,128]{1,0:T(8,128)(2,1)S(1)} collective-permute-done((bf16[2048,128]{1,0:T(8,128)(2,1)S(1)}, bf16[2048,128]{1,0:T(8,128)(2,1)S(1)}, u32[]{:S(2)}, u32[]{:S(2)}) %collective-permute-start) | collective-permute-done | bytes 524320 | tf_op jit(solution)/shard_map/ppermute | solution.py:21
  50.6 0.3 collective-permute-done.1
  50.9 1.5 %pad_maximum_fusion = bf16[8192,128]{1,0:T(8,128)(2,1)S(1)} fusion(bf16[2048,128]{1,0:T(8,128)(2,1)} %collective-permute-done.1, bf16[4096,128]{1,0:T(8,128)(2,1)} %param.12, bf16[2048,128]{1,0:T(8,128)(2,1)S(1)} %collective-permute-done), kind=kLoop, calls=%fused_computation.7 | loop fusion | flops 6291456 | bytes 4194304 | tf_op jit(solution)/shard_map/concatenate | solution.py:23
  52.4 6.7 %gather_fusion = bf16[128,256,128]{2,1,0:T(8,128)(2,1)} fusion(bf16[32,256,128]{2,1,0:T(8,128)(2,1)S(1)} %bitcast.52, s32[1024]{0:T(1024)S(1)} %pad_clamp_fusion.2), kind=kCustom, calls=%fused_computation | custom fusion | bytes 16777728 | tf_op jit(solution)/shard_map/gather | solution.py:57
  59.1 0.0 copy-start.11
  59.1 0.0 copy-start.6
  59.1 0.0 copy-start.5
  59.1 12.0 %copy.28 = bf16[128,256,128]{1,2,0:T(8,128)(2,1)} copy(bf16[128,256,128]{2,1,0:T(8,128)(2,1)} %gather_fusion) | data formatting | bytes 16777216 | tf_op jit(solution)/shard_map/gather | solution.py:57
  71.2 1.4 %fusion.34 = (bf16[32,64,128]{2,1,0:T(8,128)(2,1)S(1)}, bf16[32,64,128]{2,1,0:T(8,128)(2,1)S(1)}) fusion(bf16[32,128,128]{2,1,0:T(8,128)(2,1)} %all-gather.5.cloned.1.call-done), kind=kLoop, calls=%fused_computation.63 | loop fusion | bytes 2097152 | tf_op jit(solution)/shard_map/split | solution.py:9
  72.6 0.0 copy-done.11
  72.6 0.4 convolution_convert_fusion.2
  73.0 0.4 convolution_convert_fusion.1
  73.4 0.0 copy-done.6
  73.4 0.0 copy-done.7
  73.4 0.4 fusion.11
  73.8 0.0 copy-done.4
  73.8 0.0 copy-done.5
  73.9 0.4 convolution_bitcast_fusion.1
  74.3 0.2 copy.35
  74.5 0.0 copy-done.2
  74.5 0.0 copy-done.3
  74.5 1.9 %fusion.9 = f32[16,128,256]{2,1,0:T(8,128)} fusion(bf16[16,64,256]{2,1,0:T(8,128)(2,1)S(1)} %copy-done, f32[16,64,128]{2,1,0:T(8,128)S(1)} %bitcast.57, bf16[16,64,256]{2,1,0:T(8,128)(2,1)S(1)} %copy-done.3, bf16[16,256,128]{2,1,0:T(8,128)(2,1)S(1)} %bitcast.56), kind=kOutput, calls=%fused_computation.15 | convolution fusion | flops 134479872 | bytes 4718592 | tf_op jit(solution)/shard_map/lrk,lrc->lkc/dot_general | solution.py:108
  76.4 25.2 %all-gather.3.cloned.1.call-done = bf16[16,8,256,256]{3,2,1,0:T(8,128)(2,1)} async-done(((bf16[16,4,256,256]{3,2,1,0:T(8,128)(2,1)}), bf16[16,8,256,256]{3,2,1,0:T(8,128)(2,1)}) %all-gather.3.cloned.1.call-update) | async-done | bytes 16777232 | tf_op jit(solution)/shard_map/all_gather | solution.py:54
  101.6 11.9 %fusion.4 = f32[16,256,128]{1,2,0:T(8,128)S(1)} fusion(f32[16,128,256]{2,1,0:T(8,128)} %fusion.9, bf16[16,8,256,256]{3,2,1,0:T(8,128)(2,1)} %all-gather.3.cloned.1.call-done, bf16[16,8,256,128]{2,3,1,0:T(8,128)(2,1)} %bitcast.54, pred[16,8]{1,0:T(8,128)(4,1)S(1)} %iota_compare_fusion), kind=kOutput, calls=%fused_computation.9 | convolution fusion | flops 2152202240 | bytes 29360256 | tf_op jit(solution)/shard_map/lsij,lsjc->lic/dot_general | solution.py:60
  113.6 1.8 %copy.36 = f32[16,256,128]{2,1,0:T(8,128)} copy(f32[16,256,128]{1,2,0:T(8,128)S(1)} %fusion.4) | data formatting | bytes 4194304 | tf_op jit(solution)/shard_map/add | solution.py:111
  (14 shorter events, 0.1 us)
Async XLA Ops:
  6.5 1.0 copy-start
  6.5 64.6 %all-gather.5.cloned.1.call-start = ((), (), s32[]{:S(2)}) async-start(), calls=%async_computation.1 | async-start | bytes 1114112 | tf_op jit(solution)/shard_map/all_gather | solution.py:10
  11.8 8.3 %copy-start.1 = (bf16[4096,128]{1,0:T(8,128)(2,1)S(1)}, bf16[4096,128]{1,0:T(8,128)(2,1)}, u32[]{:S(2)}) copy-start(bf16[4096,128]{1,0:T(8,128)(2,1)} %param.12) | copy-start | bytes 3145732
  11.8 14.3 %copy-start.9 = (s32[16,4]{0,1:T(4,128)S(1)}, s32[16,4]{0,1:T(4,128)}, u32[]{:S(2)}) copy-start(s32[16,4]{0,1:T(4,128)} %param.18) | copy-start | bytes 772
  11.8 14.5 %copy-start.10 = (s32[16]{0:T(128)S(1)}, s32[16]{0:T(128)}, u32[]{:S(2)}) copy-start(s32[16]{0:T(128)} %param.15) | copy-start | bytes 196
  11.8 14.6 %copy-start.8 = (s32[16,8]{0,1:T(8,128)S(1)}, s32[16,8]{0,1:T(8,128)}, u32[]{:S(2)}) copy-start(s32[16,8]{0,1:T(8,128)} %param.14) | copy-start | bytes 1540
  11.8 89.8 %all-gather.3.cloned.1.call-start = ((), (), s32[]{:S(2)}) async-start(), calls=%async_computation | async-start | bytes 25165824 | tf_op jit(solution)/shard_map/all_gather | solution.py:54
  13.2 17.0 %collective-permute-start.2 = (bf16[8,64,128]{2,1,0:T(8,128)(2,1)}, bf16[8,64,128]{2,1,0:T(8,128)(2,1)}, u32[]{:S(2)}, u32[]{:S(2)}) collective-permute-start(bf16[8,64,128]{2,1,0:T(8,128)(2,1)} %get-tuple-element.9), channel_id=1, source_target_pairs={{0,2},{2,4},{4,6},{6,8},{8,10},{10,12},{12,14},{14,16},{16,18},{18... | collective-permute-start | bytes 393224 | tf_op jit(solution)/shard_map/ppermute | solution.py:21
  18.8 11.4 %collective-permute-start.3 = (bf16[8,64,128]{2,1,0:T(8,128)(2,1)S(1)}, bf16[8,64,128]{2,1,0:T(8,128)(2,1)}, u32[]{:S(2)}, u32[]{:S(2)}) collective-permute-start(bf16[8,64,128]{2,1,0:T(8,128)(2,1)S(1)} %get-tuple-element.10), channel_id=1, source_target_pairs={{2,0},{4,2},{6,4},{8,6},{10,8},{12,10},{14,12},{16,14},{18,16},{20... | collective-permute-start | bytes 393224 | tf_op jit(solution)/shard_map/ppermute | solution.py:22
  20.1 30.5 %collective-permute-start = (bf16[2048,128]{1,0:T(8,128)(2,1)S(1)}, bf16[2048,128]{1,0:T(8,128)(2,1)S(1)}, u32[]{:S(2)}, u32[]{:S(2)}) collective-permute-start(bf16[2048,128]{1,0:T(8,128)(2,1)S(1)} %get-tuple-element.5), channel_id=1, source_target_pairs={{0,2},{2,4},{4,6},{6,8},{8,10},{10,12},{12,14},{14,16},{16,18},{18... | collective-permute-start | bytes 1572872 | tf_op jit(solution)/shard_map/ppermute | solution.py:21
  24.7 26.2 %collective-permute-start.1 = (bf16[2048,128]{1,0:T(8,128)(2,1)S(1)}, bf16[2048,128]{1,0:T(8,128)(2,1)}, u32[]{:S(2)}, u32[]{:S(2)}) collective-permute-start(bf16[2048,128]{1,0:T(8,128)(2,1)S(1)} %get-tuple-element.6), channel_id=1, source_target_pairs={{2,0},{4,2},{6,4},{8,6},{10,8},{12,10},{14,12},{16,14},{18,16},{20... | collective-permute-start | bytes 1572872 | tf_op jit(solution)/shard_map/ppermute | solution.py:22
  59.1 13.5 %copy-start.11 = (s32[32]{0:T(128)S(1)}, s32[32]{0:T(128)}, u32[]{:S(2)}) copy-start(s32[32]{0:T(128)} %and_select_fusion) | copy-start | bytes 388
  59.1 14.3 %copy-start.6 = (bf16[2,64,256]{2,1,0:T(8,128)(2,1)S(1)}, bf16[2,64,256]{2,1,0:T(8,128)(2,1)}, u32[]{:S(2)}) copy-start(bf16[2,64,256]{2,1,0:T(8,128)(2,1)} %gather_fusion.2) | copy-start | bytes 196612
  59.1 14.3 %copy-start.7 = (bf16[2,64,64]{2,1,0:T(8,128)(2,1)S(1)}, bf16[2,64,64]{2,1,0:T(8,128)(2,1)}, u32[]{:S(2)}) copy-start(bf16[2,64,64]{2,1,0:T(8,128)(2,1)} %param.22) | copy-start | bytes 49156
  59.1 14.7 %copy-start.4 = (bf16[2,64,512]{2,1,0:T(8,128)(2,1)S(1)}, bf16[2,64,512]{2,1,0:T(8,128)(2,1)}, u32[]{:S(2)}) copy-start(bf16[2,64,512]{2,1,0:T(8,128)(2,1)} %param.19) | copy-start | bytes 393220
  59.1 14.7 %copy-start.5 = (bf16[2,64,256]{2,1,0:T(8,128)(2,1)S(1)}, bf16[2,64,256]{2,1,0:T(8,128)(2,1)}, u32[]{:S(2)}) copy-start(bf16[2,64,256]{2,1,0:T(8,128)(2,1)} %param.20) | copy-start | bytes 196612
  71.2 3.3 %copy-start.2 = (bf16[64,64,128]{2,1,0:T(8,128)(2,1)S(1)}, bf16[64,64,128]{2,1,0:T(8,128)(2,1)}, u32[]{:S(2)}) copy-start(bf16[64,64,128]{2,1,0:T(8,128)(2,1)} %gather_fusion.1) | copy-start | bytes 3145732
  71.2 3.3 %copy-start.3 = (bf16[16,64,256]{2,1,0:T(8,128)(2,1)S(1)}, bf16[16,64,256]{2,1,0:T(8,128)(2,1)}, u32[]{:S(2)}) copy-start(bf16[16,64,256]{2,1,0:T(8,128)(2,1)} %param.17) | copy-start | bytes 1572868
Sparse Core Ops, SparseCore 0:
  11.9 59.2 all-gather.4
  72.7 28.8 all-gather.2
